TPU v7x, 128 devices: a whole 4x4x4 slice. The times are simulated.
128 devices in a mesh: light: 8 (over z, core), view: 16 (over x, y).
Axes of the slice: x: 4, y: 4, z: 4, core: 2. Of those that a mesh axis runs over, the one named last changes fastest.
Arguments:
- density: bfloat16 [2048, 64, 1024], P('view', None, 'light'), may hold values from 0 to 8, as said below
- color_coef: float32 [3, 4], replicated, may hold values from 0.2 to 1
Outputs:
- image: float32 [3, 64, 1024], P(None, 'view', 'light')
Inputs may be any that keep to these rules, and one draw needn't show every extreme that they name: `density`: densities are nonnegative.
All inputs are finite; a program needn't handle non-finite values.
Results may differ from a plain program's by a relative error of at most 0.0003.
Values sent between devices are 32-bit elements; how exact they have to be, the bound alone decides.
A program may use at most 64 MiB of HBM per device.

v0:
```python
import jax
import jax.numpy as jnp
from jax import lax
from jax.sharding import PartitionSpec as P


def shifted(x, axis, by):
    devices = lax.axis_size(axis)
    pairs = [(i, i + by) for i in range(devices) if 0 <= i + by < devices]
    return lax.ppermute(x, axis, pairs)


def composite(pieces):
    depths = pieces[:, 3]
    before = jnp.cumsum(depths, axis=0) - depths
    return jnp.sum(pieces[:, :3] * jnp.exp(-before)[:, None], axis=0)


def body(density, color_coef):
    values = density.astype(jnp.float32)
    view_cells = values.shape[0]
    planes = values.shape[1]
    light_cells = values.shape[2]
    light_count = lax.axis_size("light")
    view_count = lax.axis_size("view")
    total_light = light_cells * light_count
    total_view = view_cells * view_count
    light_step = 2.0 / total_light * values
    light_run = jnp.cumsum(light_step, axis=2)
    sheet_total = light_run[:, :, -1]
    view_step = 2.0 / total_view * values
    view_run = jnp.cumsum(view_step, axis=0)
    alpha = 1.0 - jnp.exp(-view_step)
    coef = color_coef[:, :, None, None, None]
    palette = coef[:, 0] + values[None] * (
        coef[:, 1] + values[None] * (coef[:, 2] + values[None] * coef[:, 3])
    )
    upstream = jnp.zeros_like(sheet_total)
    for hop_index in range(light_count - 1):
        upstream = shifted(upstream + sheet_total, "light", 1)
    lit = jnp.exp(-(upstream[:, :, None] + light_run - light_step))
    weight = alpha * (0.3 + lit) * jnp.exp(-(view_run - view_step))
    partial_value = jnp.sum(palette * weight[None], axis=1)
    depth_sheet = view_run[-1]
    row_count = planes // view_count
    stacked = jnp.concatenate([partial_value, depth_sheet[None]], axis=0)[None]
    every = lax.all_gather(stacked, "view", axis=0, tiled=True)
    whole_image = composite(every)
    picture = lax.dynamic_slice_in_dim(
        whole_image, lax.axis_index("view") * row_count, row_count, 1
    )
    return picture


def solution(mesh):
    placed = (P("view", None, "light"), P())
    return jax.shard_map(
        body, mesh=mesh, in_specs=placed, out_specs=P(None, "view", "light"), check_vma=False
    )
```

profile of v0, /device:TPU:96, one launch (start us, length us, event | category | flops | bytes accessed | tf_op | source)
XLA Modules:
  0.0 136.0 jit_solution(15067752554143854435)
XLA Ops:
  6.5 0.0 all-gather.3.cloned.1.call-start
  6.5 3.8 %copy.18 = bf16[128,64,128]{0,1,2:T(8,128)(2,1)S(1)} copy(bf16[128,64,128]{2,1,0:T(8,128)(2,1)} %param.2) | data formatting | bytes 4194304 | tf_op args[0]
  10.4 0.5 fusion
  10.8 0.0 copy-start
  10.9 1.9 %collective-permute-start = (f32[128,64]{0,1:T(8,128)S(1)}, f32[128,64]{0,1:T(8,128)S(1)}, u32[]{:S(2)}, u32[]{:S(2)}) collective-permute-start(f32[128,64]{0,1:T(8,128)S(1)} %slice_bitcast_fusion), channel_id=1, source_target_pairs={{0,16},{16,32},{32,48},{48,64},{64,80},{80,96},{96,112},{1,17},{17... | collective-permute-start | bytes 98312 | tf_op jit(solution)/shard_map/ppermute | solution.py:10
  12.8 3.3 %collective-permute-done = f32[128,64]{0,1:T(8,128)S(1)} collective-permute-done((f32[128,64]{0,1:T(8,128)S(1)}, f32[128,64]{0,1:T(8,128)S(1)}, u32[]{:S(2)}, u32[]{:S(2)}) %collective-permute-start) | collective-permute-done | bytes 32800 | tf_op jit(solution)/shard_map/ppermute | solution.py:10
  16.1 1.9 %collective-permute-start.1 = (f32[128,64]{0,1:T(8,128)S(1)}, f32[128,64]{0,1:T(8,128)S(1)}, u32[]{:S(2)}, u32[]{:S(2)}) collective-permute-start(f32[128,64]{0,1:T(8,128)S(1)} %fusion.15), channel_id=1, source_target_pairs={{0,16},{16,32},{32,48},{48,64},{64,80},{80,96},{96,112},{1,17},{17... | collective-permute-start | bytes 98312 | tf_op jit(solution)/shard_map/ppermute | solution.py:10
  18.0 3.3 %collective-permute-done.1 = f32[128,64]{0,1:T(8,128)S(1)} collective-permute-done((f32[128,64]{0,1:T(8,128)S(1)}, f32[128,64]{0,1:T(8,128)S(1)}, u32[]{:S(2)}, u32[]{:S(2)}) %collective-permute-start.1) | collective-permute-done | bytes 32800 | tf_op jit(solution)/shard_map/ppermute | solution.py:10
  21.3 1.9 %collective-permute-start.2 = (f32[128,64]{0,1:T(8,128)S(1)}, f32[128,64]{0,1:T(8,128)S(1)}, u32[]{:S(2)}, u32[]{:S(2)}) collective-permute-start(f32[128,64]{0,1:T(8,128)S(1)} %fusion.14), channel_id=1, source_target_pairs={{0,16},{16,32},{32,48},{48,64},{64,80},{80,96},{96,112},{1,17},{17... | collective-permute-start | bytes 98312 | tf_op jit(solution)/shard_map/ppermute | solution.py:10
  23.2 3.3 %collective-permute-done.2 = f32[128,64]{0,1:T(8,128)S(1)} collective-permute-done((f32[128,64]{0,1:T(8,128)S(1)}, f32[128,64]{0,1:T(8,128)S(1)}, u32[]{:S(2)}, u32[]{:S(2)}) %collective-permute-start.2) | collective-permute-done | bytes 32800 | tf_op jit(solution)/shard_map/ppermute | solution.py:10
  26.6 1.9 %collective-permute-start.3 = (f32[128,64]{0,1:T(8,128)S(1)}, f32[128,64]{0,1:T(8,128)S(1)}, u32[]{:S(2)}, u32[]{:S(2)}) collective-permute-start(f32[128,64]{0,1:T(8,128)S(1)} %fusion.13), channel_id=1, source_target_pairs={{0,16},{16,32},{32,48},{48,64},{64,80},{80,96},{96,112},{1,17},{17... | collective-permute-start | bytes 98312 | tf_op jit(solution)/shard_map/ppermute | solution.py:10
  28.5 3.3 %collective-permute-done.3 = f32[128,64]{0,1:T(8,128)S(1)} collective-permute-done((f32[128,64]{0,1:T(8,128)S(1)}, f32[128,64]{0,1:T(8,128)S(1)}, u32[]{:S(2)}, u32[]{:S(2)}) %collective-permute-start.3) | collective-permute-done | bytes 32800 | tf_op jit(solution)/shard_map/ppermute | solution.py:10
  31.8 0.0 copy-done
  31.8 1.9 %collective-permute-start.4 = (f32[128,64]{0,1:T(8,128)S(1)}, f32[128,64]{0,1:T(8,128)S(1)}, u32[]{:S(2)}, u32[]{:S(2)}) collective-permute-start(f32[128,64]{0,1:T(8,128)S(1)} %fusion.12), channel_id=1, source_target_pairs={{0,16},{16,32},{32,48},{48,64},{64,80},{80,96},{96,112},{1,17},{17... | collective-permute-start | bytes 98312 | tf_op jit(solution)/shard_map/ppermute | solution.py:10
  33.7 2.5 %convert_multiply_fusion = f32[128,64,128]{0,1,2:T(8,128)} fusion(bf16[128,64,128]{0,1,2:T(8,128)(2,1)S(1)} %copy.18), kind=kLoop, calls=%fused_computation.5 | loop fusion | flops 2097152 | bytes 6291456 | tf_op jit(solution)/shard_map/mul | solution.py:31
  36.2 5.5 %copy.20 = f32[128,64,128]{2,1,0:T(8,128)} copy(f32[128,64,128]{0,1,2:T(8,128)} %convert_multiply_fusion) | data formatting | bytes 8388608 | tf_op jit(solution)/shard_map/mul | solution.py:31
  41.7 0.0 collective-permute-done.4
  41.7 0.8 fusion.11
  42.5 0.0 copy-start.2
  42.5 2.0 %collective-permute-start.5 = (f32[128,64]{0,1:T(8,128)S(1)}, f32[128,64]{0,1:T(8,128)S(1)}, u32[]{:S(2)}, u32[]{:S(2)}) collective-permute-start(f32[128,64]{0,1:T(8,128)S(1)} %fusion.11), channel_id=1, source_target_pairs={{0,16},{16,32},{32,48},{48,64},{64,80},{80,96},{96,112},{1,17},{17... | collective-permute-start | bytes 98312 | tf_op jit(solution)/shard_map/ppermute | solution.py:10
  44.5 2.5 %fusion.16 = f32[128,64,128]{2,1,0:T(8,128)S(1)} fusion(f32[128,64,128]{2,1,0:T(8,128)} %copy.20), kind=kOutput, calls=%fused_computation.28 | output fusion | flops 133169152 | bytes 8388608 | tf_op jit(solution)/shard_map/jit(cumsum)/reduce_window_sum | solution.py:32
  47.0 0.0 copy-start.1
  47.0 0.8 collective-permute-done.5
  47.8 0.8 fusion.10
  48.6 1.9 %collective-permute-start.6 = (f32[128,64]{0,1:T(8,128)S(1)}, f32[128,64]{0,1:T(8,128)S(1)}, u32[]{:S(2)}, u32[]{:S(2)}) collective-permute-start(f32[128,64]{0,1:T(8,128)S(1)} %fusion.10), channel_id=1, source_target_pairs={{0,16},{16,32},{32,48},{48,64},{64,80},{80,96},{96,112},{1,17},{17... | collective-permute-start | bytes 98312 | tf_op jit(solution)/shard_map/ppermute | solution.py:10
  50.5 0.0 copy-done.2
  50.6 0.2 slice_reduce_fusion.3
  50.8 0.0 copy-done.1
  50.8 5.5 %copy.21 = f32[128,64,128]{0,1,2:T(8,128)} copy(f32[128,64,128]{2,1,0:T(8,128)} %copy-done.1) | data formatting | bytes 8388608 | tf_op jit(solution)/shard_map/jit(cumsum)/reduce_window_sum | solution.py:32
  56.3 3.6 %copy.19 = f32[128,64,128]{2,1,0:T(8,128)} copy(bf16[128,64,128]{0,1,2:T(8,128)(2,1)S(1)} %copy.18) | data formatting | bytes 6291456 | tf_op jit(solution)/shard_map/convert_element_type | solution.py:20
  59.9 0.0 collective-permute-done.6
  59.9 6.0 %exponential_multiply_fusion = f32[128,64,128]{0,1,2:T(8,128)} fusion(f32[128,64,128]{0,1,2:T(8,128)} %copy.21, f32[128,64,128]{0,1,2:T(8,128)} %copy-done, bf16[128,64,128]{0,1,2:T(8,128)(2,1)S(1)} %copy.18, f32[128,64]{0,1:T(8,128)S(1)} %collective-permute-done.6), kind=kLoop, calls=%fused_computation.1 | loop fusion | flops 13631488 | bytes 14712832 | tf_op jit(solution)/shard_map/mul | solution.py:42
  66.0 5.5 %copy.22 = f32[128,64,128]{2,1,0:T(8,128)} copy(f32[128,64,128]{0,1,2:T(8,128)} %exponential_multiply_fusion) | data formatting | bytes 8388608 | tf_op jit(solution)/shard_map/mul | solution.py:42
  71.4 0.0 slice-start
  71.4 5.9 %multiply_reduce_fusion = f32[3,64,128]{2,1,0:T(8,128)S(1)} fusion(f32[128,64,128]{2,1,0:T(8,128)} %copy.22, f32[3]{0:T(128)S(1)} %get-tuple-element.6, f32[3]{0:T(128)S(1)} %get-tuple-element.7, f32[3]{0:T(128)S(1)} %get-tuple-element.8, f32[128,64,128]{2,1,0:T(8,128)} %copy.19, f32[3]{0:T(128)S(1)} %get-tuple-element.5), kind=kLoop, calls=%fused_computation | loop fusion | flops 25141248 | bytes 8486960 | tf_op jit(solution)/shard_map/reduce_sum | solution.py:43
  77.3 0.0 slice-done
  77.3 0.7 pad_maximum_fusion
  78.0 0.0 all-gather.3.cloned.1.call-update
  78.0 47.4 %all-gather.3.cloned.1.call-done = f32[64,64,128]{2,1,0:T(8,128)} async-done(((f32[4,64,128]{2,1,0:T(8,128)}), f32[64,64,128]{2,1,0:T(8,128)}) %all-gather.3.cloned.1.call-update) | async-done | bytes 2097168 | tf_op jit(solution)/shard_map/all_gather | solution.py:47
  125.4 1.5 %fusion.7 = f32[16,64,128]{2,1,0:T(8,128)S(1)} fusion(f32[16,4,64,128]{3,2,1,0:T(8,128)} %bitcast.19), kind=kOutput, calls=%fused_computation.12 | output fusion | flops 2228224 | bytes 1048576 | tf_op jit(solution)/shard_map/jit(cumsum)/reduce_window_sum | solution.py:15
  126.9 1.6 %fusion.4 = f32[3,64,128]{2,1,0:T(8,128)S(1)} fusion(f32[16,4,64,128]{3,2,1,0:T(8,128)} %bitcast.20, f32[16,64,128]{2,1,0:T(8,128)S(1)} %fusion.7), kind=kLoop, calls=%fused_computation.8 | loop fusion | flops 761856 | bytes 2195456 | tf_op jit(solution)/shard_map/reduce_sum | solution.py:16
  128.6 0.6 constant_dynamic-slice_fusion
  (5 shorter events, 0.0 us)
Async XLA Ops:
  6.5 118.9 %all-gather.3.cloned.1.call-start = ((), (), s32[]{:S(2)}) async-start(), calls=%async_computation | async-start | bytes 2228224 | tf_op jit(solution)/shard_map/all_gather | solution.py:47
  10.8 20.9 %copy-start = (f32[128,64,128]{0,1,2:T(8,128)}, f32[128,64,128]{0,1,2:T(8,128)S(1)}, u32[]{:S(2)}) copy-start(f32[128,64,128]{0,1,2:T(8,128)S(1)} %fusion) | copy-start | bytes 12582916
  10.9 5.2 %collective-permute-start = (f32[128,64]{0,1:T(8,128)S(1)}, f32[128,64]{0,1:T(8,128)S(1)}, u32[]{:S(2)}, u32[]{:S(2)}) collective-permute-start(f32[128,64]{0,1:T(8,128)S(1)} %slice_bitcast_fusion), channel_id=1, source_target_pairs={{0,16},{16,32},{32,48},{48,64},{64,80},{80,96},{96,112},{1,17},{17... | collective-permute-start | bytes 98312 | tf_op jit(solution)/shard_map/ppermute | solution.py:10
  16.1 5.2 %collective-permute-start.1 = (f32[128,64]{0,1:T(8,128)S(1)}, f32[128,64]{0,1:T(8,128)S(1)}, u32[]{:S(2)}, u32[]{:S(2)}) collective-permute-start(f32[128,64]{0,1:T(8,128)S(1)} %fusion.15), channel_id=1, source_target_pairs={{0,16},{16,32},{32,48},{48,64},{64,80},{80,96},{96,112},{1,17},{17... | collective-permute-start | bytes 98312 | tf_op jit(solution)/shard_map/ppermute | solution.py:10
  21.3 5.2 %collective-permute-start.2 = (f32[128,64]{0,1:T(8,128)S(1)}, f32[128,64]{0,1:T(8,128)S(1)}, u32[]{:S(2)}, u32[]{:S(2)}) collective-permute-start(f32[128,64]{0,1:T(8,128)S(1)} %fusion.14), channel_id=1, source_target_pairs={{0,16},{16,32},{32,48},{48,64},{64,80},{80,96},{96,112},{1,17},{17... | collective-permute-start | bytes 98312 | tf_op jit(solution)/shard_map/ppermute | solution.py:10
  26.6 5.2 %collective-permute-start.3 = (f32[128,64]{0,1:T(8,128)S(1)}, f32[128,64]{0,1:T(8,128)S(1)}, u32[]{:S(2)}, u32[]{:S(2)}) collective-permute-start(f32[128,64]{0,1:T(8,128)S(1)} %fusion.13), channel_id=1, source_target_pairs={{0,16},{16,32},{32,48},{48,64},{64,80},{80,96},{96,112},{1,17},{17... | collective-permute-start | bytes 98312 | tf_op jit(solution)/shard_map/ppermute | solution.py:10
  31.8 9.9 %collective-permute-start.4 = (f32[128,64]{0,1:T(8,128)S(1)}, f32[128,64]{0,1:T(8,128)S(1)}, u32[]{:S(2)}, u32[]{:S(2)}) collective-permute-start(f32[128,64]{0,1:T(8,128)S(1)} %fusion.12), channel_id=1, source_target_pairs={{0,16},{16,32},{32,48},{48,64},{64,80},{80,96},{96,112},{1,17},{17... | collective-permute-start | bytes 98312 | tf_op jit(solution)/shard_map/ppermute | solution.py:10
  42.5 8.1 %copy-start.2 = (f32[3,4]{1,0:T(4,128)S(1)}, f32[3,4]{1,0:T(4,128)}, u32[]{:S(2)}) copy-start(f32[3,4]{1,0:T(4,128)} %param.3) | copy-start | bytes 148
  42.5 5.4 %collective-permute-start.5 = (f32[128,64]{0,1:T(8,128)S(1)}, f32[128,64]{0,1:T(8,128)S(1)}, u32[]{:S(2)}, u32[]{:S(2)}) collective-permute-start(f32[128,64]{0,1:T(8,128)S(1)} %fusion.11), channel_id=1, source_target_pairs={{0,16},{16,32},{32,48},{48,64},{64,80},{80,96},{96,112},{1,17},{17... | collective-permute-start | bytes 98312 | tf_op jit(solution)/shard_map/ppermute | solution.py:10
  47.0 3.7 %copy-start.1 = (f32[128,64,128]{2,1,0:T(8,128)}, f32[128,64,128]{2,1,0:T(8,128)S(1)}, u32[]{:S(2)}) copy-start(f32[128,64,128]{2,1,0:T(8,128)S(1)} %fusion.16) | copy-start | bytes 12582916
  48.6 11.3 %collective-permute-start.6 = (f32[128,64]{0,1:T(8,128)S(1)}, f32[128,64]{0,1:T(8,128)S(1)}, u32[]{:S(2)}, u32[]{:S(2)}) collective-permute-start(f32[128,64]{0,1:T(8,128)S(1)} %fusion.10), channel_id=1, source_target_pairs={{0,16},{16,32},{32,48},{48,64},{64,80},{80,96},{96,112},{1,17},{17... | collective-permute-start | bytes 98312 | tf_op jit(solution)/shard_map/ppermute | solution.py:10
  71.4 5.9 %slice-start = ((f32[128,64,128]{2,1,0:T(8,128)}), f32[1,64,128]{2,1,0:T(8,128)S(1)}, s32[]{:S(2)}) async-start(f32[128,64,128]{2,1,0:T(8,128)} %copy-done.1), calls=%async_computation.1 | async-start | bytes 65536 | tf_op jit(solution)/shard_map/slice | solution.py:44
Sparse Core Ops, SparseCore 0:
  78.1 47.2 all-gather.2
where the time goes:
time: 138 us; the launch traced here: 136 us
  waiting for transfers between devices  61.4 us (44%)
  local copies, waits for them, and re-layouts  24.7 us (18%)
  other arithmetic  22.9 us (17%)
  starting transfers between devices  13.5 us (10%)
  between operations  13.5 us (10%)
    all_gather x1, waiting for transfers between devices, body(): every = lax.all_gather(stacked, 'view', axis=0, tiled=True)  47.4 us
    ppermute x7, waiting for transfers between devices, shifted(): return lax.ppermute(x, axis, pairs)  14 us
    ppermute x7, starting transfers between devices, shifted(): return lax.ppermute(x, axis, pairs)  13.5 us
    mul x1, other arithmetic, body(): weight = alpha * (0.3 + lit) * jnp.exp(-(view_run - view_step))  6.04 us
    reduce_sum x1, other arithmetic, body(): partial_value = jnp.sum(palette * weight[None], axis=1)  5.88 us
    another operation x1, local copies, waits for them, and re-layouts, body(): view_run = jnp.cumsum(view_step, axis=0)  5.49 us
    mul x1, local copies, waits for them, and re-layouts, body(): weight = alpha * (0.3 + lit) * jnp.exp(-(view_run - view_step))  5.47 us
    mul x1, local copies, waits for them, and re-layouts, body(): view_step = 2.0 / total_view * values  5.46 us
  transfers between devices with their start and end apart: 8, of which 6 were waited for; matrix products, arithmetic and copies ran while one was open for 15% of the time, Pallas kernels for 0%

commit v1 on v0

v1 whole, which is shorter than its diff:
```python
import functools
import math

import jax
import jax.numpy as jnp
from jax import lax
from jax.experimental import pallas as pl
from jax.experimental.pallas import tpu as pltpu
from jax.sharding import PartitionSpec as P

F32 = jnp.float32
BF16 = jnp.bfloat16
LOG2E = math.log2(math.e)
ROWS = 16
BLOCK = 16
TURN = (2, 1, 3, 0)


def kernel(
    light_total, view_total, light_count, view_count, far,
    x_hbm, coef_hbm, out_ref,
    xv, coef_s, own_sum, sib_sum, chip_sum, low_sum, upper, lit_alpha, base, piece, got,
    x_sem, coef_sem, sib_send, sib_recv, low_send, low_recv, piece_send, piece_recv,
):
    li = lax.axis_index("light")
    vi = lax.axis_index("view")
    chip, core = li // 2, li % 2
    chips = light_count // 2
    cells = x_hbm.shape[0]
    lanes = x_hbm.shape[2]
    planes = x_hbm.shape[1]
    chunks = planes // ROWS
    rows = planes // view_count
    per_chunk = ROWS // rows
    vx = vi // per_chunk

    def load(k):
        z0 = pl.multiple_of(((vx + TURN[k]) % chunks) * ROWS, ROWS)
        return pltpu.make_async_copy(x_hbm.at[:, pl.ds(z0, ROWS), :], xv.at[k], x_sem.at[k])

    def sib_copy(k):
        return pltpu.make_async_remote_copy(
            src_ref=own_sum.at[k], dst_ref=sib_sum.at[k], send_sem=sib_send.at[k], recv_sem=sib_recv.at[k],
            device_id=(chip * 2 + 1, vi), device_id_type=pl.DeviceIdType.MESH)

    def low_copy(k, to_chip, to_core):
        return pltpu.make_async_remote_copy(
            src_ref=chip_sum.at[k], dst_ref=low_sum.at[chip, k],
            send_sem=low_send.at[to_chip - 1, to_core, k], recv_sem=low_recv.at[chip, k],
            device_id=(to_chip * 2 + to_core, vi), device_id_type=pl.DeviceIdType.MESH)

    def low_arrival(k, from_chip):
        return pltpu.make_async_remote_copy(
            src_ref=chip_sum.at[k], dst_ref=low_sum.at[from_chip, k],
            send_sem=low_send.at[0, 0, k], recv_sem=low_recv.at[from_chip, k],
            device_id=(from_chip * 2 + 1, vi), device_id_type=pl.DeviceIdType.MESH)

    def piece_copy(k, d, j):
        return pltpu.make_async_remote_copy(
            src_ref=piece.at[k, d], dst_ref=got.at[vi], send_sem=piece_send.at[k, d], recv_sem=piece_recv.at[vi],
            device_id=(li, j), device_id_type=pl.DeviceIdType.MESH)

    def piece_arrival(i):
        return pltpu.make_async_remote_copy(
            src_ref=piece.at[0, 0], dst_ref=got.at[i], send_sem=piece_send.at[0, 0], recv_sem=piece_recv.at[i],
            device_id=(li, (vi + 1) % view_count), device_id_type=pl.DeviceIdType.MESH)

    for k in range(chunks):
        load(k).start()
    coef_copy = pltpu.make_async_copy(coef_hbm, coef_s, coef_sem)
    coef_copy.start()

    barrier = pltpu.get_barrier_semaphore()
    for other in range(1, view_count):
        pl.semaphore_signal(barrier, inc=1, device_id=(li, (vi + other) % view_count), device_id_type=pl.DeviceIdType.MESH)

    @pl.when(core == 1)
    def _():
        pl.semaphore_signal(barrier, inc=1, device_id=(li - 1, vi), device_id_type=pl.DeviceIdType.MESH)

    for c in range(chips - 1):
        @pl.when(c < chip)
        def _():
            pl.semaphore_signal(barrier, inc=1, device_id=(2 * c + 1, vi), device_id_type=pl.DeviceIdType.MESH)

    lane = lax.broadcasted_iota(jnp.int32, (ROWS, lanes), 1)
    r = lax.broadcasted_iota(jnp.int32, (lanes, lanes), 0)
    c = lax.broadcasted_iota(jnp.int32, (lanes, lanes), 1)
    before = jnp.where(r < c, 1.0, 0.0).astype(BF16)
    ones = jnp.ones((lanes, lanes), BF16)

    def block_of(k, b):
        return xv[k, pl.ds(b * BLOCK, BLOCK)].reshape(BLOCK * ROWS, lanes)

    for k in range(chunks):
        load(k).wait()

        def gather(b, acc):
            total = jnp.dot(block_of(k, b), ones, preferred_element_type=F32).reshape(BLOCK, ROWS, lanes)
            for v in range(BLOCK):
                acc = jnp.where(lane == b * BLOCK + v, total[v], acc)
            return acc

        own_sum[k] = lax.fori_loop(0, cells // BLOCK, gather, jnp.zeros((ROWS, lanes), F32))
        if k == 0:
            pl.semaphore_wait(barrier, (view_count - 1) + jnp.where(core == 0, 1, 2 * (chips - 1 - chip)))

        @pl.when(core == 0)
        def _():
            sib_copy(k).start()

    @pl.when(core == 1)
    def _():
        for k in range(chunks):
            sib_copy(k).wait_recv()
            chip_sum[k] = own_sum[k] + sib_sum[k]
            for to_chip in range(1, chips):
                @pl.when(to_chip > chip)
                def _():
                    for to_core in range(2):
                        low_copy(k, to_chip, to_core).start()

    view_scale = -LOG2E * 2.0 / view_total
    light_scale = -LOG2E * 2.0 / light_total
    for k in range(chunks):
        def local(b, carry):
            clear, m0, m1, m2, m3 = carry
            xb = block_of(k, b)
            depth = jnp.dot(xb, before, preferred_element_type=F32).reshape(BLOCK, ROWS, lanes)
            xb = xb.reshape(BLOCK, ROWS, lanes)
            for v in range(BLOCK):
                x = xb[v].astype(F32)
                beyond = clear * jnp.exp2(view_scale * x)
                a = clear - beyond
                clear = beyond
                lit_alpha[k, b * BLOCK + v] = a * jnp.exp2(light_scale * depth[v])
                m0 = m0 + a
                a = a * x
                m1 = m1 + a
                a = a * x
                m2 = m2 + a
                a = a * x
                m3 = m3 + a
            return clear, m0, m1, m2, m3

        zero = jnp.zeros((ROWS, lanes), F32)
        clear, *sums = lax.fori_loop(0, cells // BLOCK, local, (jnp.ones((ROWS, lanes), F32), zero, zero, zero, zero))
        base[k, 4] = clear
        for i in range(4):
            base[k, i] = 0.3 * sums[i]

    coef_copy.wait()
    for k in range(chunks):
        upper[...] = jnp.zeros_like(upper)

        @pl.when(core == 1)
        def _():
            upper[...] += sib_sum[k]

        for c in range(chips - 1):
            @pl.when(c < chip)
            def _():
                low_arrival(k, c).wait_recv()
                upper[...] += low_sum[c, k]

        dim = jnp.exp2(light_scale * upper[...])

        def lighted(b, carry):
            m0, m1, m2, m3 = carry
            near = pltpu.roll(dim, (lanes - b * BLOCK) % lanes, 1)
            xb = xv[k, pl.ds(b * BLOCK, BLOCK)]
            for v in range(BLOCK):
                x = xb[v].astype(F32)
                a = lit_alpha[k, b * BLOCK + v] * jnp.broadcast_to(near[:, v : v + 1], (ROWS, lanes))
                m0 = m0 + a
                a = a * x
                m1 = m1 + a
                a = a * x
                m2 = m2 + a
                a = a * x
                m3 = m3 + a
            return m0, m1, m2, m3

        sums = lax.fori_loop(0, cells // BLOCK, lighted, tuple(base[k, i] for i in range(4)))
        parts = [
            coef_s[ch, 0] * sums[0] + coef_s[ch, 1] * sums[1] + coef_s[ch, 2] * sums[2] + coef_s[ch, 3] * sums[3]
            for ch in range(3)
        ] + [base[k, 4]]
        to = ((vx + TURN[k]) % chunks) * per_chunk
        for d in range(per_chunk):
            mine = jnp.concatenate([p[d * rows : (d + 1) * rows] for p in parts], axis=0)
            piece[k, d] = mine
            j = to + d

            @pl.when(j == vi)
            def _():
                got[vi] = mine

            @pl.when(j != vi)
            def _():
                piece_copy(k, d, j).start()

    for i in range(view_count):
        @pl.when(i != vi)
        def _():
            piece_arrival(i).wait_recv()

    clear = jnp.ones((rows, lanes), F32)
    total = [jnp.zeros((rows, lanes), F32) for _ in range(3)]
    for i in range(view_count):
        for ch in range(3):
            total[ch] = total[ch] + clear * got[i, ch * rows : (ch + 1) * rows]
        clear = clear * got[i, 3 * rows : 4 * rows]
    for ch in range(3):
        out_ref[ch] = total[ch]

    @pl.when(core == 0)
    def _():
        for k in range(chunks):
            sib_copy(k).wait_send()

    @pl.when(core == 1)
    def _():
        for k in range(chunks):
            for to_chip in range(1, chips):
                @pl.when(to_chip > chip)
                def _():
                    for to_core in range(2):
                        low_copy(k, to_chip, to_core).wait_send()

    for k in range(chunks):
        to = ((vx + TURN[k]) % chunks) * per_chunk
        for d in range(per_chunk):
            @pl.when(to + d != vi)
            def _():
                piece_copy(k, d, to + d).wait_send()


def body(density, color_coef):
    cells, planes, lanes = density.shape
    light_count = lax.axis_size("light")
    view_count = lax.axis_size("view")
    chips = light_count // 2
    chunks = planes // ROWS
    rows = planes // view_count
    per_chunk = ROWS // rows
    dma = pltpu.SemaphoreType.DMA
    return pl.pallas_call(
        functools.partial(kernel, lanes * light_count, cells * view_count, light_count, view_count, None),
        out_shape=jax.ShapeDtypeStruct((3, rows, lanes), F32),
        in_specs=[pl.BlockSpec(memory_space=pl.ANY), pl.BlockSpec(memory_space=pl.ANY)],
        out_specs=pl.BlockSpec(memory_space=pltpu.VMEM),
        scratch_shapes=[
            pltpu.VMEM((chunks, cells, ROWS, lanes), BF16),
            pltpu.SMEM((3, 4), F32),
            pltpu.VMEM((chunks, ROWS, lanes), F32),
            pltpu.VMEM((chunks, ROWS, lanes), F32),
            pltpu.VMEM((chunks, ROWS, lanes), F32),
            pltpu.VMEM((chips - 1, chunks, ROWS, lanes), F32),
            pltpu.VMEM((ROWS, lanes), F32),
            pltpu.VMEM((chunks, cells, ROWS, lanes), F32),
            pltpu.VMEM((chunks, 5, ROWS, lanes), F32),
            pltpu.VMEM((chunks, per_chunk, 4 * rows, lanes), F32),
            pltpu.VMEM((view_count, 4 * rows, lanes), F32),
            dma((chunks,)),
            dma,
            dma((chunks,)),
            dma((chunks,)),
            dma((chips - 1, 2, chunks)),
            dma((chips - 1, chunks)),
            dma((chunks, per_chunk)),
            dma((view_count,)),
        ],
        compiler_params=pltpu.CompilerParams(collective_id=0, has_side_effects=True),
    )(density, color_coef)


def solution(mesh):
    placed = (P("view", None, "light"), P())
    return jax.shard_map(
        body, mesh=mesh, in_specs=placed, out_specs=P(None, "view", "light"), check_vma=False
    )
```

time: 138 us -> 28.6 us (0.21)
  the two profiles are of different devices: /device:TPU:96 before, /device:TPU:1 now
where the time goes in v1:
time: 28.6 us; the launch traced here: 28.4 us
  Pallas kernels  27.1 us (95%)
  local copies, waits for them, and re-layouts  1.29 us (5%)
    pallas_call x1, Pallas kernels, body(): pl.pallas_call(functools.partial(kernel, lanes * light_count, cells * vie...  27.1 us
    unnamed x1, local copies, waits for them, and re-layouts  1.29 us

profile of v1, /device:TPU:1, one launch (start us, length us, event | category | flops | bytes accessed | tf_op | source)
XLA Modules:
  0.0 28.4 jit_solution(4040312455491113597)
XLA Ops:
  0.0 27.1 %shard_map.28 = f32[3,4,128]{2,1,0:T(4,128)} custom-call(bf16[128,64,128]{2,1,0:T(8,128)(2,1)} %x_hbm.1, f32[3,4]{1,0:T(4,128)} %coef_hbm.1), custom_call_target="tpu_custom_call" | custom-call | tf_op jit(solution)/shard_map/pallas_call | solution.py:248
  27.1 1.3 %copy.4 = f32[3,4,128]{2,1,0:T(4,128)} copy(f32[3,4,128]{2,1,0:T(4,128)} %shard_map.28) | data formatting | bytes 12288

commit v2 on v1

v2 whole, which is shorter than its diff:
```python
import functools
import math

import jax
import jax.numpy as jnp
from jax import lax
from jax.experimental import pallas as pl
from jax.experimental.pallas import tpu as pltpu
from jax.sharding import PartitionSpec as P

F32 = jnp.float32
BF16 = jnp.bfloat16
LOG2E = math.log2(math.e)
ROWS = 16
BLOCK = 16
HALF = BLOCK // 2
TURN = (2, 1, 3, 0)
AMBIENT = 0.3
MESH = pl.DeviceIdType.MESH


def kernel(
    light_total, view_total, light_count, view_count,
    x_hbm, coef_hbm, out_ref,
    xv, coef_s, own_sum, sib_sum, chip_sum, low_sum, upper, dim_t, dims, xf, alpha, lit_alpha, clears, piece, got,
    x_sem, coef_sem, sib_send, sib_recv, low_send, low_recv, piece_send, piece_recv,
):
    li = lax.axis_index("light")
    vi = lax.axis_index("view")
    chip, core = li // 2, li % 2
    chips = light_count // 2
    cells, planes, lanes = x_hbm.shape
    chunks = planes // ROWS
    rows = planes // view_count
    per_chunk = ROWS // rows
    steps = cells // BLOCK
    vx = vi // per_chunk

    def load(k):
        z0 = pl.multiple_of(((vx + TURN[k]) % chunks) * ROWS, ROWS)
        return pltpu.make_async_copy(x_hbm.at[:, pl.ds(z0, ROWS), :], xv.at[k], x_sem.at[k])

    def sib_copy(k):
        return pltpu.make_async_remote_copy(
            src_ref=own_sum.at[k], dst_ref=sib_sum.at[k], send_sem=sib_send.at[k], recv_sem=sib_recv.at[k],
            device_id=(chip * 2 + 1, vi), device_id_type=MESH)

    def low_copy(k, to_chip, to_core):
        return pltpu.make_async_remote_copy(
            src_ref=chip_sum.at[k], dst_ref=low_sum.at[chip, k],
            send_sem=low_send.at[to_chip - 1, to_core, k], recv_sem=low_recv.at[chip, k],
            device_id=(to_chip * 2 + to_core, vi), device_id_type=MESH)

    def low_arrival(k, from_chip):
        return pltpu.make_async_remote_copy(
            src_ref=chip_sum.at[k], dst_ref=low_sum.at[from_chip, k],
            send_sem=low_send.at[0, 0, k], recv_sem=low_recv.at[from_chip, k],
            device_id=(from_chip * 2 + 1, vi), device_id_type=MESH)

    def piece_copy(k, d, j):
        return pltpu.make_async_remote_copy(
            src_ref=piece.at[k, d], dst_ref=got.at[vi], send_sem=piece_send, recv_sem=piece_recv,
            device_id=(li, j), device_id_type=MESH)

    def all_pieces():
        others = pl.ds(0, view_count - 1)
        return pltpu.make_async_remote_copy(
            src_ref=got.at[others], dst_ref=got.at[others], send_sem=piece_send, recv_sem=piece_recv,
            device_id=(li, (vi + 1) % view_count), device_id_type=MESH)

    for k in range(chunks):
        load(k).start()
    coef_copy = pltpu.make_async_copy(coef_hbm, coef_s, coef_sem)
    coef_copy.start()

    barrier = pltpu.get_barrier_semaphore()

    @pl.when(core == 1)
    def _():
        pl.semaphore_signal(barrier, inc=1, device_id=(li - 1, vi), device_id_type=MESH)

    for c in range(chips - 1):
        @pl.when(c < chip)
        def _():
            pl.semaphore_signal(barrier, inc=1, device_id=(2 * c + 1, vi), device_id_type=MESH)

    for other in range(1, view_count):
        pl.semaphore_signal(barrier, inc=1, device_id=(li, (vi + other) % view_count), device_id_type=MESH)

    row = lax.broadcasted_iota(jnp.int32, (ROWS, lanes), 0)
    for k in range(chunks):
        load(k).wait()
        acc = jnp.zeros((steps, BLOCK * ROWS), F32)
        for p in range(steps):
            xb = xv[k, p * BLOCK : (p + 1) * BLOCK].reshape(BLOCK * ROWS, lanes)
            pick = jnp.where(row == p, 1.0, 0.0).astype(BF16)[:steps]
            acc = acc + lax.dot_general(pick, xb, (((1,), (1,)), ((), ())), preferred_element_type=F32)
        own_sum[k, 0:steps] = acc[:, : HALF * ROWS]
        own_sum[k, steps:] = acc[:, HALF * ROWS :]
        if k == 0:
            pl.semaphore_wait(barrier, (view_count - 1) + jnp.where(core == 0, 1, 2 * (chips - 1 - chip)))

        @pl.when(core == 0)
        def _():
            sib_copy(k).start()

    @pl.when(core == 1)
    def _():
        for k in range(chunks):
            sib_copy(k).wait_recv()
            chip_sum[k] = own_sum[k] + sib_sum[k]
            for to_chip in range(1, chips):
                @pl.when(to_chip > chip)
                def _():
                    for to_core in range(2):
                        low_copy(k, to_chip, to_core).start()

    view_scale = -LOG2E * 2.0 / view_total
    light_scale = -LOG2E * 2.0 / light_total
    r = lax.broadcasted_iota(jnp.int32, (lanes, lanes), 0)
    c = lax.broadcasted_iota(jnp.int32, (lanes, lanes), 1)
    before = jnp.where(r < c, 1.0, 0.0).astype(BF16)
    for k in range(chunks):
        def local(b, clear):
            xb = xv[k, pl.ds(b * BLOCK, BLOCK)].reshape(BLOCK * ROWS, lanes)
            depth = jnp.dot(xb, before, preferred_element_type=F32).reshape(BLOCK, ROWS, lanes)
            xb = xb.reshape(BLOCK, ROWS, lanes)
            for v in range(BLOCK):
                x = xb[v].astype(F32)
                beyond = clear * jnp.exp2(view_scale * x)
                a = clear - beyond
                clear = beyond
                xf[k, b * BLOCK + v] = x
                alpha[k, b * BLOCK + v] = a
                lit_alpha[k, b * BLOCK + v] = a * jnp.exp2(light_scale * depth[v])
            return clear

        clears[k] = lax.fori_loop(0, steps, local, jnp.ones((ROWS, lanes), F32))

    coef_copy.wait()
    for k in range(chunks):
        upper[...] = jnp.zeros_like(upper)

        @pl.when(core == 1)
        def _():
            upper[...] += sib_sum[k]

        for c in range(chips - 1):
            @pl.when(c < chip)
            def _():
                low_arrival(k, c).wait_recv()
                upper[...] += low_sum[c, k]

        dim_t[...] = jnp.transpose(jnp.exp2(light_scale * upper[...]) * (1.0 / AMBIENT))

        def spread(p):
            for h in range(2):
                at = jnp.full((HALF * ROWS, 2 * steps), h * steps, jnp.int32) + p
                near = jnp.take_along_axis(dim_t[...], jnp.broadcast_to(at[:, :1], (HALF * ROWS, lanes)), axis=1)
                dims[p % 2, h * HALF : (h + 1) * HALF] = near.reshape(HALF, ROWS, lanes)

        def lighted(p, carry):
            m0, m1, m2, m3 = carry
            spread(p)
            for v in range(BLOCK):
                x = xf[k, p * BLOCK + v]
                a = alpha[k, p * BLOCK + v] + lit_alpha[k, p * BLOCK + v] * dims[p % 2, v]
                m0 = m0 + a
                a = a * x
                m1 = m1 + a
                a = a * x
                m2 = m2 + a
                a = a * x
                m3 = m3 + a
            return m0, m1, m2, m3

        zero = jnp.zeros((ROWS, lanes), F32)
        sums = lax.fori_loop(0, steps, lighted, (zero, zero, zero, zero))
        parts = []
        for ch in range(3):
            t = coef_s[ch, 0] * sums[0] + coef_s[ch, 1] * sums[1] + coef_s[ch, 2] * sums[2] + coef_s[ch, 3] * sums[3]
            parts.append(AMBIENT * t)
        parts.append(clears[k])
        to = ((vx + TURN[k]) % chunks) * per_chunk
        for d in range(per_chunk):
            mine = jnp.concatenate([p[d * rows : (d + 1) * rows] for p in parts], axis=0)
            piece[k, d] = mine
            j = to + d

            @pl.when(j == vi)
            def _():
                got[vi] = mine

            @pl.when(j != vi)
            def _():
                piece_copy(k, d, j).start()

    all_pieces().wait_recv()
    half = lax.broadcasted_iota(jnp.int32, (2 * rows, lanes), 0)
    clear = jnp.ones((2 * rows, lanes), F32)
    total = [jnp.zeros((2 * rows, lanes), F32) for _ in range(2)]
    for i in range(view_count):
        first, second = got[i, : 2 * rows], got[i, 2 * rows :]
        total[0] = total[0] + clear * first
        total[1] = total[1] + clear * second
        clear = clear * jnp.where(half < rows, pltpu.roll(second, rows, 0), second)
    out_ref[0] = total[0][:rows]
    out_ref[1] = total[0][rows:]
    out_ref[2] = total[1][:rows]

    all_pieces().wait_send()

    @pl.when(core == 0)
    def _():
        for k in range(chunks):
            sib_copy(k).wait_send()

    @pl.when(core == 1)
    def _():
        for k in range(chunks):
            for to_chip in range(1, chips):
                @pl.when(to_chip > chip)
                def _():
                    for to_core in range(2):
                        low_copy(k, to_chip, to_core).wait_send()


def body(density, color_coef):
    cells, planes, lanes = density.shape
    light_count = lax.axis_size("light")
    view_count = lax.axis_size("view")
    chips = light_count // 2
    chunks = planes // ROWS
    rows = planes // view_count
    per_chunk = ROWS // rows
    dma = pltpu.SemaphoreType.DMA
    return pl.pallas_call(
        functools.partial(kernel, lanes * light_count, cells * view_count, light_count, view_count),
        out_shape=jax.ShapeDtypeStruct((3, rows, lanes), F32),
        in_specs=[pl.BlockSpec(memory_space=pl.ANY), pl.BlockSpec(memory_space=pl.ANY)],
        out_specs=pl.BlockSpec(memory_space=pltpu.VMEM),
        scratch_shapes=[
            pltpu.VMEM((chunks, cells, ROWS, lanes), BF16),
            pltpu.SMEM((3, 4), F32),
            pltpu.VMEM((chunks, ROWS, lanes), F32),
            pltpu.VMEM((chunks, ROWS, lanes), F32),
            pltpu.VMEM((chunks, ROWS, lanes), F32),
            pltpu.VMEM((chips - 1, chunks, ROWS, lanes), F32),
            pltpu.VMEM((ROWS, lanes), F32),
            pltpu.VMEM((HALF * ROWS, ROWS), F32),
            pltpu.VMEM((2, BLOCK, ROWS, lanes), F32),
            pltpu.VMEM((chunks, cells, ROWS, lanes), F32),
            pltpu.VMEM((chunks, cells, ROWS, lanes), F32),
            pltpu.VMEM((chunks, cells, ROWS, lanes), F32),
            pltpu.VMEM((chunks, ROWS, lanes), F32),
            pltpu.VMEM((chunks, per_chunk, 4 * rows, lanes), F32),
            pltpu.VMEM((view_count, 4 * rows, lanes), F32),
            dma((chunks,)),
            dma,
            dma((chunks,)),
            dma((chunks,)),
            dma((chips - 1, 2, chunks)),
            dma((chips - 1, chunks)),
            dma,
            dma,
        ],
        compiler_params=pltpu.CompilerParams(collective_id=0, has_side_effects=True),
    )(density, color_coef)


def solution(mesh):
    placed = (P("view", None, "light"), P())
    return jax.shard_map(
        body, mesh=mesh, in_specs=placed, out_specs=P(None, "view", "light"), check_vma=False
    )
```

time: 28.6 us -> 23.1 us (0.81)
  Pallas kernels: 27.1 us -> 21.7 us
    pallas_call x1, Pallas kernels: 27.1 us -> 21.7 us  [body(): pl.pallas_call(functools.partial(kernel, lanes * light_count, cells * vie...]
where the time goes in v2:
time: 23.1 us; the launch traced here: 23 us
  Pallas kernels  21.7 us (94%)
  local copies, waits for them, and re-layouts  1.29 us (6%)
    pallas_call x1, Pallas kernels, body(): pl.pallas_call(functools.partial(kernel, lanes * light_count, cells * vie...  21.7 us
    unnamed x1, local copies, waits for them, and re-layouts  1.29 us

profile of v2, /device:TPU:1, one launch (start us, length us, event | category | flops | bytes accessed | tf_op | source)
XLA Modules:
  0.0 23.0 jit_solution(521729928681248739)
XLA Ops:
  0.0 21.7 %shard_map.28 = f32[3,4,128]{2,1,0:T(4,128)} custom-call(bf16[128,64,128]{2,1,0:T(8,128)(2,1)} %x_hbm.1, f32[3,4]{1,0:T(4,128)} %coef_hbm.1), custom_call_target="tpu_custom_call" | custom-call | tf_op jit(solution)/shard_map/pallas_call | solution.py:237
  21.7 1.3 %copy.4 = f32[3,4,128]{2,1,0:T(4,128)} copy(f32[3,4,128]{2,1,0:T(4,128)} %shard_map.28) | data formatting | bytes 12288

commit v3 on v2

--- a/solution.py
+++ b/solution.py
@@ -16,6 +16,7 @@
 HALF = BLOCK // 2
 TURN = (2, 1, 3, 0)
 AMBIENT = 0.3
+ORDER = ("A0123", "M", "S0123", "L0", "C0123", "L12", "W", "B0", "L3", "B123")
 MESH = pl.DeviceIdType.MESH
 
 
@@ -88,7 +89,7 @@
         pl.semaphore_signal(barrier, inc=1, device_id=(li, (vi + other) % view_count), device_id_type=MESH)
 
     row = lax.broadcasted_iota(jnp.int32, (ROWS, lanes), 0)
-    for k in range(chunks):
+    def sum_up(k):
         load(k).wait()
         acc = jnp.zeros((steps, BLOCK * ROWS), F32)
         for p in range(steps):
@@ -97,30 +98,34 @@
             acc = acc + lax.dot_general(pick, xb, (((1,), (1,)), ((), ())), preferred_element_type=F32)
         own_sum[k, 0:steps] = acc[:, : HALF * ROWS]
         own_sum[k, steps:] = acc[:, HALF * ROWS :]
-        if k == 0:
-            pl.semaphore_wait(barrier, (view_count - 1) + jnp.where(core == 0, 1, 2 * (chips - 1 - chip)))
-
+
+    def meet():
+        pl.semaphore_wait(barrier, (view_count - 1) + jnp.where(core == 0, 1, 2 * (chips - 1 - chip)))
+
+    def share(ks):
         @pl.when(core == 0)
         def _():
-            sib_copy(k).start()
-
-    @pl.when(core == 1)
-    def _():
-        for k in range(chunks):
-            sib_copy(k).wait_recv()
-            chip_sum[k] = own_sum[k] + sib_sum[k]
-            for to_chip in range(1, chips):
-                @pl.when(to_chip > chip)
-                def _():
-                    for to_core in range(2):
-                        low_copy(k, to_chip, to_core).start()
+            for k in ks:
+                sib_copy(k).start()
+
+    def lower(ks):
+        @pl.when(core == 1)
+        def _():
+            for k in ks:
+                sib_copy(k).wait_recv()
+                chip_sum[k] = own_sum[k] + sib_sum[k]
+                for to_chip in range(1, chips):
+                    @pl.when(to_chip > chip)
+                    def _():
+                        for to_core in range(2):
+                            low_copy(k, to_chip, to_core).start()
 
     view_scale = -LOG2E * 2.0 / view_total
     light_scale = -LOG2E * 2.0 / light_total
     r = lax.broadcasted_iota(jnp.int32, (lanes, lanes), 0)
     c = lax.broadcasted_iota(jnp.int32, (lanes, lanes), 1)
     before = jnp.where(r < c, 1.0, 0.0).astype(BF16)
-    for k in range(chunks):
+    def near_side(k):
         def local(b, clear):
             xb = xv[k, pl.ds(b * BLOCK, BLOCK)].reshape(BLOCK * ROWS, lanes)
             depth = jnp.dot(xb, before, preferred_element_type=F32).reshape(BLOCK, ROWS, lanes)
@@ -135,10 +140,9 @@
                 lit_alpha[k, b * BLOCK + v] = a * jnp.exp2(light_scale * depth[v])
             return clear
 
-        clears[k] = lax.fori_loop(0, steps, local, jnp.ones((ROWS, lanes), F32))
-
-    coef_copy.wait()
-    for k in range(chunks):
+        clears[k] = lax.fori_loop(0, steps, local, jnp.ones((ROWS, lanes), F32), unroll=8)
+
+    def light_up(k):
         upper[...] = jnp.zeros_like(upper)
 
         @pl.when(core == 1)
@@ -175,7 +179,7 @@
             return m0, m1, m2, m3
 
         zero = jnp.zeros((ROWS, lanes), F32)
-        sums = lax.fori_loop(0, steps, lighted, (zero, zero, zero, zero))
+        sums = lax.fori_loop(0, steps, lighted, (zero, zero, zero, zero), unroll=8)
         parts = []
         for ch in range(3):
             t = coef_s[ch, 0] * sums[0] + coef_s[ch, 1] * sums[1] + coef_s[ch, 2] * sums[2] + coef_s[ch, 3] * sums[3]
@@ -194,6 +198,18 @@
             @pl.when(j != vi)
             def _():
                 piece_copy(k, d, j).start()
+
+    for step in ORDER:
+        name, ks = step[0], [int(q) for q in step[1:]]
+        if name == "M":
+            meet()
+        elif name == "W":
+            coef_copy.wait()
+        elif name in "SC":
+            (share if name == "S" else lower)(ks)
+        else:
+            for k in ks:
+                {"A": sum_up, "L": near_side, "B": light_up}[name](k)
 
     all_pieces().wait_recv()
     half = lax.broadcasted_iota(jnp.int32, (2 * rows, lanes), 0)
@@ -236,7 +252,7 @@
     dma = pltpu.SemaphoreType.DMA
     return pl.pallas_call(
         functools.partial(kernel, lanes * light_count, cells * view_count, light_count, view_count),
-        out_shape=jax.ShapeDtypeStruct((3, rows, lanes), F32),
+        out_shape=pltpu.VMEM((3, rows, lanes), F32),
         in_specs=[pl.BlockSpec(memory_space=pl.ANY), pl.BlockSpec(memory_space=pl.ANY)],
         out_specs=pl.BlockSpec(memory_space=pltpu.VMEM),
         scratch_shapes=[

time: 23.1 us -> 15.6 us (0.68)
  the two profiles are of different devices: /device:TPU:1 before, /device:TPU:96 now
where the time goes in v3:
time: 15.6 us; the launch traced here: 15.5 us
  Pallas kernels  14.9 us (96%)
  local copies, waits for them, and re-layouts  0.6 us (4%)
    pallas_call x1, Pallas kernels, body(): pl.pallas_call(functools.partial(kernel, lanes * light_count, cells * vie...  14.9 us
    unnamed x1, local copies, waits for them, and re-layouts  0.6 us

profile of v3, /device:TPU:96, one launch (start us, length us, event | category | flops | bytes accessed | tf_op | source)
XLA Modules:
  0.0 15.5 jit_solution(10598830413142213649)
XLA Ops:
  0.0 14.9 %shard_map.28 = f32[3,4,128]{2,1,0:T(4,128)S(1)} custom-call(bf16[128,64,128]{2,1,0:T(8,128)(2,1)} %x_hbm.1, f32[3,4]{1,0:T(4,128)} %coef_hbm.1), custom_call_target="tpu_custom_call" | custom-call | tf_op jit(solution)/shard_map/pallas_call | solution.py:253
  14.9 0.6 %copy.4 = f32[3,4,128]{2,1,0:T(4,128)} copy(f32[3,4,128]{2,1,0:T(4,128)S(1)} %shard_map.28) | data formatting | bytes 12288

commit v4 on v3

--- a/solution.py
+++ b/solution.py
@@ -16,15 +16,15 @@
 HALF = BLOCK // 2
 TURN = (2, 1, 3, 0)
 AMBIENT = 0.3
-ORDER = ("A0123", "M", "S0123", "L0", "C0123", "L12", "W", "B0", "L3", "B123")
+ORDER = ("A0123", "L0", "M", "S0123", "L1", "C0123", "L23", "W", "B0123")
 MESH = pl.DeviceIdType.MESH
 
 
 def kernel(
     light_total, view_total, light_count, view_count,
     x_hbm, coef_hbm, out_ref,
-    xv, coef_s, own_sum, sib_sum, chip_sum, low_sum, upper, dim_t, dims, xf, alpha, lit_alpha, clears, piece, got,
-    x_sem, coef_sem, sib_send, sib_recv, low_send, low_recv, piece_send, piece_recv,
+    xv, coef_s, own_sum, sib_sum, chip_sum, low_sum, upper, picks, alpha, lit_alpha, clears, piece, got,
+    x_sem, coef_sem, sib_send, sib_recv, low_send, low_recv, piece_send, piece_recv, lines,
 ):
     li = lax.axis_index("light")
     vi = lax.axis_index("view")
@@ -35,7 +35,7 @@
     rows = planes // view_count
     per_chunk = ROWS // rows
     steps = cells // BLOCK
-    vx = vi // per_chunk
+    vx, vy = vi // per_chunk, vi % per_chunk
 
     def load(k):
         z0 = pl.multiple_of(((vx + TURN[k]) % chunks) * ROWS, ROWS)
@@ -85,8 +85,13 @@
         def _():
             pl.semaphore_signal(barrier, inc=1, device_id=(2 * c + 1, vi), device_id_type=MESH)
 
-    for other in range(1, view_count):
-        pl.semaphore_signal(barrier, inc=1, device_id=(li, (vi + other) % view_count), device_id_type=MESH)
+    for turn in range(1, chunks):
+        for j in (((vx + turn) % chunks) * per_chunk + vy, vx * per_chunk + (vy + turn) % per_chunk):
+            pl.semaphore_signal(barrier, inc=1, device_id=(li, j), device_id_type=MESH)
+
+    term_row = lax.broadcasted_iota(jnp.int32, (3 * ROWS, lanes), 0) % ROWS
+    for q in range(ROWS):
+        picks[q] = jnp.where(term_row == q, 1.0, 0.0).astype(BF16)
 
     row = lax.broadcasted_iota(jnp.int32, (ROWS, lanes), 0)
     def sum_up(k):
@@ -100,7 +105,10 @@
         own_sum[k, steps:] = acc[:, HALF * ROWS :]
 
     def meet():
-        pl.semaphore_wait(barrier, (view_count - 1) + jnp.where(core == 0, 1, 2 * (chips - 1 - chip)))
+        pl.semaphore_wait(barrier, chunks + per_chunk - 2 + jnp.where(core == 0, 1, 2 * (chips - 1 - chip)))
+        for turn in range(1, per_chunk):
+            j = vx * per_chunk + (vy + turn) % per_chunk
+            pl.semaphore_signal(lines, inc=1, device_id=(li, j), device_id_type=MESH)
 
     def share(ks):
         @pl.when(core == 0)
@@ -135,7 +143,6 @@
                 beyond = clear * jnp.exp2(view_scale * x)
                 a = clear - beyond
                 clear = beyond
-                xf[k, b * BLOCK + v] = x
                 alpha[k, b * BLOCK + v] = a
                 lit_alpha[k, b * BLOCK + v] = a * jnp.exp2(light_scale * depth[v])
             return clear
@@ -155,36 +162,36 @@
                 low_arrival(k, c).wait_recv()
                 upper[...] += low_sum[c, k]
 
-        dim_t[...] = jnp.transpose(jnp.exp2(light_scale * upper[...]) * (1.0 / AMBIENT))
-
-        def spread(p):
+        rest = jnp.exp2(light_scale * upper[...]) * (1.0 / AMBIENT)
+        terms = []
+        for _ in range(3):
+            term = rest.astype(BF16).astype(F32)
+            rest = rest - term
+            terms.append(term)
+        dim_t = jnp.transpose(jnp.concatenate(terms, axis=0)).astype(BF16)
+        m0, m1, m2, m3 = (jnp.zeros((ROWS, lanes), F32) for _ in range(4))
+        for p in range(steps):
             for h in range(2):
-                at = jnp.full((HALF * ROWS, 2 * steps), h * steps, jnp.int32) + p
-                near = jnp.take_along_axis(dim_t[...], jnp.broadcast_to(at[:, :1], (HALF * ROWS, lanes)), axis=1)
-                dims[p % 2, h * HALF : (h + 1) * HALF] = near.reshape(HALF, ROWS, lanes)
-
-        def lighted(p, carry):
-            m0, m1, m2, m3 = carry
-            spread(p)
-            for v in range(BLOCK):
-                x = xf[k, p * BLOCK + v]
-                a = alpha[k, p * BLOCK + v] + lit_alpha[k, p * BLOCK + v] * dims[p % 2, v]
-                m0 = m0 + a
-                a = a * x
-                m1 = m1 + a
-                a = a * x
-                m2 = m2 + a
-                a = a * x
-                m3 = m3 + a
-            return m0, m1, m2, m3
-
-        zero = jnp.zeros((ROWS, lanes), F32)
-        sums = lax.fori_loop(0, steps, lighted, (zero, zero, zero, zero), unroll=8)
+                near = jnp.dot(dim_t, picks[p + h * steps], preferred_element_type=F32).reshape(HALF, ROWS, lanes)
+                for i in range(HALF):
+                    v = p * BLOCK + h * HALF + i
+                    x = xv[k, v].astype(F32)
+                    a = alpha[k, v] + lit_alpha[k, v] * near[i]
+                    m0 = m0 + a
+                    a = a * x
+                    m1 = m1 + a
+                    a = a * x
+                    m2 = m2 + a
+                    a = a * x
+                    m3 = m3 + a
+        sums = (m0, m1, m2, m3)
         parts = []
         for ch in range(3):
             t = coef_s[ch, 0] * sums[0] + coef_s[ch, 1] * sums[1] + coef_s[ch, 2] * sums[2] + coef_s[ch, 3] * sums[3]
             parts.append(AMBIENT * t)
         parts.append(clears[k])
+        if k == 0:
+            pl.semaphore_wait(lines, per_chunk - 1)
         to = ((vx + TURN[k]) % chunks) * per_chunk
         for d in range(per_chunk):
             mine = jnp.concatenate([p[d * rows : (d + 1) * rows] for p in parts], axis=0)
@@ -263,9 +270,7 @@
             pltpu.VMEM((chunks, ROWS, lanes), F32),
             pltpu.VMEM((chips - 1, chunks, ROWS, lanes), F32),
             pltpu.VMEM((ROWS, lanes), F32),
-            pltpu.VMEM((HALF * ROWS, ROWS), F32),
-            pltpu.VMEM((2, BLOCK, ROWS, lanes), F32),
-            pltpu.VMEM((chunks, cells, ROWS, lanes), F32),
+            pltpu.VMEM((ROWS, 3 * ROWS, lanes), BF16),
             pltpu.VMEM((chunks, cells, ROWS, lanes), F32),
             pltpu.VMEM((chunks, cells, ROWS, lanes), F32),
             pltpu.VMEM((chunks, ROWS, lanes), F32),
@@ -279,6 +284,7 @@
             dma((chips - 1, chunks)),
             dma,
             dma,
+            pltpu.SemaphoreType.REGULAR,
         ],
         compiler_params=pltpu.CompilerParams(collective_id=0, has_side_effects=True),
     )(density, color_coef)

time: 15.6 us -> 15.1 us (0.968)
  Pallas kernels: 14.9 us -> 14.3 us
    pallas_call x1, Pallas kernels: 14.9 us -> 14.3 us  [body(): pl.pallas_call(functools.partial(kernel, lanes * light_count, cells * vie...]
where the time goes in v4:
time: 15.1 us; the launch traced here: 14.9 us
  Pallas kernels  14.3 us (95%)
  local copies, waits for them, and re-layouts  0.6 us (4%)
    pallas_call x1, Pallas kernels, body(): pl.pallas_call(functools.partial(kernel, lanes * light_count, cells * vie...  14.3 us
    unnamed x1, local copies, waits for them, and re-layouts  0.6 us

profile of v4, /device:TPU:96, one launch (start us, length us, event | category | flops | bytes accessed | tf_op | source)
XLA Modules:
  0.0 14.9 jit_solution(4268220221611652414)
XLA Ops:
  0.0 14.3 %shard_map.28 = f32[3,4,128]{2,1,0:T(4,128)S(1)} custom-call(bf16[128,64,128]{2,1,0:T(8,128)(2,1)} %x_hbm.1, f32[3,4]{1,0:T(4,128)} %coef_hbm.1), custom_call_target="tpu_custom_call" | custom-call | tf_op jit(solution)/shard_map/pallas_call | solution.py:260
  14.3 0.6 %copy.4 = f32[3,4,128]{2,1,0:T(4,128)} copy(f32[3,4,128]{2,1,0:T(4,128)S(1)} %shard_map.28) | data formatting | bytes 12288

commit v5 on v4

--- a/solution.py
+++ b/solution.py
@@ -14,9 +14,10 @@
 ROWS = 16
 BLOCK = 16
 HALF = BLOCK // 2
-TURN = (2, 1, 3, 0)
+TURN = (0, 1, 3, 2)
+GROUPS = ((0, 1), (1, 3))
 AMBIENT = 0.3
-ORDER = ("A0123", "L0", "M", "S0123", "L1", "C0123", "L23", "W", "B0123")
+ORDER = ("A0123", "L0", "M", "S", "L1", "D1", "D2", "D3", "L23", "W", "B0123")
 MESH = pl.DeviceIdType.MESH
 
 
@@ -38,25 +39,28 @@
     vx, vy = vi // per_chunk, vi % per_chunk
 
     def load(k):
-        z0 = pl.multiple_of(((vx + TURN[k]) % chunks) * ROWS, ROWS)
+        z0 = TURN[k] * ROWS
         return pltpu.make_async_copy(x_hbm.at[:, pl.ds(z0, ROWS), :], xv.at[k], x_sem.at[k])
 
-    def sib_copy(k):
-        return pltpu.make_async_remote_copy(
-            src_ref=own_sum.at[k], dst_ref=sib_sum.at[k], send_sem=sib_send.at[k], recv_sem=sib_recv.at[k],
+    def sib_copy(g):
+        ks = pl.ds(*GROUPS[g])
+        return pltpu.make_async_remote_copy(
+            src_ref=own_sum.at[ks], dst_ref=sib_sum.at[ks], send_sem=sib_send.at[g], recv_sem=sib_recv.at[g],
             device_id=(chip * 2 + 1, vi), device_id_type=MESH)
 
-    def low_copy(k, to_chip, to_core):
-        return pltpu.make_async_remote_copy(
-            src_ref=chip_sum.at[k], dst_ref=low_sum.at[chip, k],
-            send_sem=low_send.at[to_chip - 1, to_core, k], recv_sem=low_recv.at[chip, k],
-            device_id=(to_chip * 2 + to_core, vi), device_id_type=MESH)
-
-    def low_arrival(k, from_chip):
-        return pltpu.make_async_remote_copy(
-            src_ref=chip_sum.at[k], dst_ref=low_sum.at[from_chip, k],
-            send_sem=low_send.at[0, 0, k], recv_sem=low_recv.at[from_chip, k],
-            device_id=(from_chip * 2 + 1, vi), device_id_type=MESH)
+    def low_copy(g, by, to_core):
+        ks = pl.ds(*GROUPS[g])
+        return pltpu.make_async_remote_copy(
+            src_ref=chip_sum.at[ks], dst_ref=low_sum.at[chip, ks],
+            send_sem=low_send.at[by - 1, to_core, g], recv_sem=low_recv.at[chip, g],
+            device_id=((chip + by) * 2 + to_core, vi), device_id_type=MESH)
+
+    def low_arrival(g, c):
+        ks = pl.ds(*GROUPS[g])
+        return pltpu.make_async_remote_copy(
+            src_ref=chip_sum.at[ks], dst_ref=low_sum.at[c, ks],
+            send_sem=low_send.at[0, 0, g], recv_sem=low_recv.at[c, g],
+            device_id=(c * 2 + 1, vi), device_id_type=MESH)
 
     def piece_copy(k, d, j):
         return pltpu.make_async_remote_copy(
@@ -106,27 +110,30 @@
 
     def meet():
         pl.semaphore_wait(barrier, chunks + per_chunk - 2 + jnp.where(core == 0, 1, 2 * (chips - 1 - chip)))
+
         for turn in range(1, per_chunk):
             j = vx * per_chunk + (vy + turn) % per_chunk
             pl.semaphore_signal(lines, inc=1, device_id=(li, j), device_id_type=MESH)
 
-    def share(ks):
+    def share():
         @pl.when(core == 0)
         def _():
-            for k in ks:
-                sib_copy(k).start()
-
-    def lower(ks):
-        @pl.when(core == 1)
-        def _():
-            for k in ks:
-                sib_copy(k).wait_recv()
-                chip_sum[k] = own_sum[k] + sib_sum[k]
-                for to_chip in range(1, chips):
-                    @pl.when(to_chip > chip)
-                    def _():
-                        for to_core in range(2):
-                            low_copy(k, to_chip, to_core).start()
+            for g in range(len(GROUPS)):
+                sib_copy(g).start()
+
+    def lower(by):
+        if by == 1:
+            @pl.when(core == 1)
+            def _():
+                for g in range(len(GROUPS)):
+                    sib_copy(g).wait_recv()
+                chip_sum[...] = own_sum[...] + sib_sum[...]
+
+        @pl.when((core == 1) & (chip + by < chips))
+        def _():
+            for g in range(len(GROUPS)):
+                for to_core in range(2):
+                    low_copy(g, by, to_core).start()
 
     view_scale = -LOG2E * 2.0 / view_total
     light_scale = -LOG2E * 2.0 / light_total
@@ -150,16 +157,19 @@
         clears[k] = lax.fori_loop(0, steps, local, jnp.ones((ROWS, lanes), F32), unroll=8)
 
     def light_up(k):
-        upper[...] = jnp.zeros_like(upper)
+        @pl.when(core == 0)
+        def _():
+            upper[...] = jnp.zeros_like(upper)
 
         @pl.when(core == 1)
         def _():
-            upper[...] += sib_sum[k]
+            upper[...] = sib_sum[k]
 
         for c in range(chips - 1):
             @pl.when(c < chip)
             def _():
-                low_arrival(k, c).wait_recv()
+                if k < len(GROUPS):
+                    low_arrival(k, c).wait_recv()
                 upper[...] += low_sum[c, k]
 
         rest = jnp.exp2(light_scale * upper[...]) * (1.0 / AMBIENT)
@@ -192,7 +202,7 @@
         parts.append(clears[k])
         if k == 0:
             pl.semaphore_wait(lines, per_chunk - 1)
-        to = ((vx + TURN[k]) % chunks) * per_chunk
+        to = TURN[k] * per_chunk
         for d in range(per_chunk):
             mine = jnp.concatenate([p[d * rows : (d + 1) * rows] for p in parts], axis=0)
             piece[k, d] = mine
@@ -206,17 +216,14 @@
             def _():
                 piece_copy(k, d, j).start()
 
+    one = {"M": meet, "S": share, "W": coef_copy.wait}
+    each = {"A": sum_up, "D": lower, "L": near_side, "B": light_up}
     for step in ORDER:
-        name, ks = step[0], [int(q) for q in step[1:]]
-        if name == "M":
-            meet()
-        elif name == "W":
-            coef_copy.wait()
-        elif name in "SC":
-            (share if name == "S" else lower)(ks)
+        if step in one:
+            one[step]()
         else:
-            for k in ks:
-                {"A": sum_up, "L": near_side, "B": light_up}[name](k)
+            for q in step[1:]:
+                each[step[0]](int(q))
 
     all_pieces().wait_recv()
     half = lax.broadcasted_iota(jnp.int32, (2 * rows, lanes), 0)
@@ -235,17 +242,15 @@
 
     @pl.when(core == 0)
     def _():
-        for k in range(chunks):
-            sib_copy(k).wait_send()
-
-    @pl.when(core == 1)
-    def _():
-        for k in range(chunks):
-            for to_chip in range(1, chips):
-                @pl.when(to_chip > chip)
-                def _():
-                    for to_core in range(2):
-                        low_copy(k, to_chip, to_core).wait_send()
+        for g in range(len(GROUPS)):
+            sib_copy(g).wait_send()
+
+    for by in range(1, chips):
+        @pl.when((core == 1) & (chip + by < chips))
+        def _():
+            for g in range(len(GROUPS)):
+                for to_core in range(2):
+                    low_copy(g, by, to_core).wait_send()
 
 
 def body(density, color_coef):
@@ -278,10 +283,10 @@
             pltpu.VMEM((view_count, 4 * rows, lanes), F32),
             dma((chunks,)),
             dma,
-            dma((chunks,)),
-            dma((chunks,)),
-            dma((chips - 1, 2, chunks)),
-            dma((chips - 1, chunks)),
+            dma((len(GROUPS),)),
+            dma((len(GROUPS),)),
+            dma((chips - 1, 2, len(GROUPS))),
+            dma((chips - 1, len(GROUPS))),
             dma,
             dma,
             pltpu.SemaphoreType.REGULAR,

time: 15.1 us -> 14.8 us (0.980)
  the two profiles are of different devices: /device:TPU:96 before, /device:TPU:68 now
where the time goes in v5:
time: 14.8 us; the launch traced here: 14.7 us
  Pallas kernels  14 us (95%)
  local copies, waits for them, and re-layouts  0.6 us (4%)
    pallas_call x1, Pallas kernels, body(): pl.pallas_call(functools.partial(kernel, lanes * light_count, cells * vie...  14 us
    unnamed x1, local copies, waits for them, and re-layouts  0.6 us

profile of v5, /device:TPU:68, one launch (start us, length us, event | category | flops | bytes accessed | tf_op | source)
XLA Modules:
  0.0 14.7 jit_solution(11497173857380338590)
XLA Ops:
  0.0 14.0 %shard_map.28 = f32[3,4,128]{2,1,0:T(4,128)S(1)} custom-call(bf16[128,64,128]{2,1,0:T(8,128)(2,1)} %x_hbm.1, f32[3,4]{1,0:T(4,128)} %coef_hbm.1), custom_call_target="tpu_custom_call" | custom-call | tf_op jit(solution)/shard_map/pallas_call | solution.py:265
  14.1 0.6 %copy.4 = f32[3,4,128]{2,1,0:T(4,128)} copy(f32[3,4,128]{2,1,0:T(4,128)S(1)} %shard_map.28) | data formatting | bytes 12288

commit v6 on v5

--- a/solution.py
+++ b/solution.py
@@ -14,17 +14,17 @@
 ROWS = 16
 BLOCK = 16
 HALF = BLOCK // 2
+HROWS = ROWS // 2
 TURN = (0, 1, 3, 2)
 GROUPS = ((0, 1), (1, 3))
 AMBIENT = 0.3
-ORDER = ("A0123", "L0", "M", "S", "L1", "D1", "D2", "D3", "L23", "W", "B0123")
 MESH = pl.DeviceIdType.MESH
 
 
 def kernel(
     light_total, view_total, light_count, view_count,
     x_hbm, coef_hbm, out_ref,
-    xv, coef_s, own_sum, sib_sum, chip_sum, low_sum, upper, picks, alpha, lit_alpha, clears, piece, got,
+    xv, coef_s, own_sum, sib_sum, chip_sum, low_sum, upper, picks, dims, alpha, lit_alpha, clears, piece, got,
     x_sem, coef_sem, sib_send, sib_recv, low_send, low_recv, piece_send, piece_recv, lines,
 ):
     li = lax.axis_index("light")
@@ -156,74 +156,105 @@
 
         clears[k] = lax.fori_loop(0, steps, local, jnp.ones((ROWS, lanes), F32), unroll=8)
 
-    def light_up(k):
+    def arrive(g):
+        first, count = GROUPS[g]
+        ks = pl.ds(first, count)
+
         @pl.when(core == 0)
         def _():
-            upper[...] = jnp.zeros_like(upper)
+            upper[ks] = jnp.zeros((count, ROWS, lanes), F32)
 
         @pl.when(core == 1)
         def _():
-            upper[...] = sib_sum[k]
+            upper[ks] = sib_sum[ks]
 
         for c in range(chips - 1):
             @pl.when(c < chip)
             def _():
-                if k < len(GROUPS):
-                    low_arrival(k, c).wait_recv()
-                upper[...] += low_sum[c, k]
-
-        rest = jnp.exp2(light_scale * upper[...]) * (1.0 / AMBIENT)
-        terms = []
-        for _ in range(3):
-            term = rest.astype(BF16).astype(F32)
-            rest = rest - term
-            terms.append(term)
-        dim_t = jnp.transpose(jnp.concatenate(terms, axis=0)).astype(BF16)
-        m0, m1, m2, m3 = (jnp.zeros((ROWS, lanes), F32) for _ in range(4))
+                low_arrival(g, c).wait_recv()
+                upper[ks] += low_sum[c, ks]
+
+        for k in range(first, first + count):
+            rest = jnp.exp2(light_scale * upper[k]) * (1.0 / AMBIENT)
+            terms = []
+            for _ in range(3):
+                term = rest.astype(BF16).astype(F32)
+                rest = rest - term
+                terms.append(term)
+            turned = jnp.transpose(jnp.concatenate(terms, axis=0))
+            for z in range(2):
+                part = [turned[i * ROWS + z * HROWS : i * ROWS + (z + 1) * HROWS] for i in range(HALF)]
+                dims[k, z] = jnp.concatenate(part, axis=0).astype(BF16)
+
+    def nearness(k, z, q):
+        return jnp.dot(dims[k, z], picks[q], preferred_element_type=F32).reshape(HALF, HROWS, lanes)
+
+    ahead = {}
+
+    def light_up(k, z, then=None):
+        zs = slice(z * HROWS, (z + 1) * HROWS)
+        sums = [[jnp.zeros((HROWS, lanes), F32) for _ in range(4)] for _ in range(2)]
         for p in range(steps):
             for h in range(2):
-                near = jnp.dot(dim_t, picks[p + h * steps], preferred_element_type=F32).reshape(HALF, ROWS, lanes)
+                q = p + h * steps
+                near = ahead.pop((k, z), None) if q == 0 else None
+                near = nearness(k, z, q) if near is None else near
                 for i in range(HALF):
                     v = p * BLOCK + h * HALF + i
-                    x = xv[k, v].astype(F32)
-                    a = alpha[k, v] + lit_alpha[k, v] * near[i]
-                    m0 = m0 + a
-                    a = a * x
-                    m1 = m1 + a
-                    a = a * x
-                    m2 = m2 + a
-                    a = a * x
-                    m3 = m3 + a
-        sums = (m0, m1, m2, m3)
+                    x = xv[k, v].astype(F32)[zs]
+                    a = alpha[k, v, zs] + lit_alpha[k, v, zs] * near[i]
+                    acc = sums[i % 2]
+                    for power in range(4):
+                        acc[power] = acc[power] + a
+                        if power < 3:
+                            a = a * x
+        if then is not None:
+            ahead[then] = nearness(*then, 0)
+        m0, m1, m2, m3 = (even + odd for even, odd in zip(*sums))
         parts = []
         for ch in range(3):
-            t = coef_s[ch, 0] * sums[0] + coef_s[ch, 1] * sums[1] + coef_s[ch, 2] * sums[2] + coef_s[ch, 3] * sums[3]
+            t = coef_s[ch, 0] * m0 + coef_s[ch, 1] * m1 + coef_s[ch, 2] * m2 + coef_s[ch, 3] * m3
             parts.append(AMBIENT * t)
-        parts.append(clears[k])
-        if k == 0:
+        parts.append(clears[k, zs])
+        if k == 0 and z == 0:
             pl.semaphore_wait(lines, per_chunk - 1)
-        to = TURN[k] * per_chunk
-        for d in range(per_chunk):
-            mine = jnp.concatenate([p[d * rows : (d + 1) * rows] for p in parts], axis=0)
+        half = per_chunk // 2
+        for d in range(z * half, (z + 1) * half):
+            j = TURN[k] * per_chunk + d
+            first = (d - z * half) * rows
+            mine = jnp.concatenate([p[first : first + rows] for p in parts], axis=0)
             piece[k, d] = mine
-            j = to + d
-
-            @pl.when(j == vi)
-            def _():
-                got[vi] = mine
+            got[jnp.where(j == vi, vi, view_count)] = mine
+        for d in range(z * half, (z + 1) * half):
+            j = TURN[k] * per_chunk + d
 
             @pl.when(j != vi)
             def _():
                 piece_copy(k, d, j).start()
 
-    one = {"M": meet, "S": share, "W": coef_copy.wait}
-    each = {"A": sum_up, "D": lower, "L": near_side, "B": light_up}
-    for step in ORDER:
-        if step in one:
-            one[step]()
-        else:
-            for q in step[1:]:
-                each[step[0]](int(q))
+    def low_chips():
+        meet()
+        for by in range(1, chips):
+            lower(by)
+
+    for k in range(chunks):
+        sum_up(k)
+    pl.when(core == 0)(meet)
+    share()
+    near_side(0)
+    near_side(1)
+    pl.when((core == 1) & (chip > 0))(low_chips)
+    near_side(2)
+    pl.when((core == 1) & (chip == 0))(low_chips)
+    coef_copy.wait()
+    near_side(3)
+    arrive(0)
+    light_up(0, 0, (0, 1))
+    light_up(0, 1)
+    arrive(1)
+    halves = ((1, 0), (2, 0), (1, 1), (3, 0), (2, 1), (3, 1))
+    for half, then in zip(halves, halves[1:] + (None,)):
+        light_up(*half, then)
 
     all_pieces().wait_recv()
     half = lax.broadcasted_iota(jnp.int32, (2 * rows, lanes), 0)
@@ -274,13 +305,14 @@
             pltpu.VMEM((chunks, ROWS, lanes), F32),
             pltpu.VMEM((chunks, ROWS, lanes), F32),
             pltpu.VMEM((chips - 1, chunks, ROWS, lanes), F32),
-            pltpu.VMEM((ROWS, lanes), F32),
+            pltpu.VMEM((chunks, ROWS, lanes), F32),
             pltpu.VMEM((ROWS, 3 * ROWS, lanes), BF16),
+            pltpu.VMEM((chunks, 2, lanes // 2, 3 * ROWS), BF16),
             pltpu.VMEM((chunks, cells, ROWS, lanes), F32),
             pltpu.VMEM((chunks, cells, ROWS, lanes), F32),
             pltpu.VMEM((chunks, ROWS, lanes), F32),
             pltpu.VMEM((chunks, per_chunk, 4 * rows, lanes), F32),
-            pltpu.VMEM((view_count, 4 * rows, lanes), F32),
+            pltpu.VMEM((view_count + 1, 4 * rows, lanes), F32),
             dma((chunks,)),
             dma,
             dma((len(GROUPS),)),

time: 14.8 us -> 14.3 us (0.966)
  the two profiles are of different devices: /device:TPU:68 before, /device:TPU:96 now
where the time goes in v6:
time: 14.3 us; the launch traced here: 14 us
  Pallas kernels  13.4 us (94%)
  local copies, waits for them, and re-layouts  0.6 us (4%)
    pallas_call x1, Pallas kernels, body(): pl.pallas_call(functools.partial(kernel, lanes * light_count, cells * vie...  13.4 us
    unnamed x1, local copies, waits for them, and re-layouts  0.6 us

profile of v6, /device:TPU:96, one launch (start us, length us, event | category | flops | bytes accessed | tf_op | source)
XLA Modules:
  0.0 14.0 jit_solution(5493740248011105874)
XLA Ops:
  0.0 13.4 %shard_map.28 = f32[3,4,128]{2,1,0:T(4,128)S(1)} custom-call(bf16[128,64,128]{2,1,0:T(8,128)(2,1)} %x_hbm.1, f32[3,4]{1,0:T(4,128)} %coef_hbm.1), custom_call_target="tpu_custom_call" | custom-call | tf_op jit(solution)/shard_map/pallas_call | solution.py:296
  13.4 0.6 %copy.4 = f32[3,4,128]{2,1,0:T(4,128)} copy(f32[3,4,128]{2,1,0:T(4,128)S(1)} %shard_map.28) | data formatting | bytes 12288

commit v7 on v6

--- a/solution.py
+++ b/solution.py
@@ -116,24 +116,20 @@
             pl.semaphore_signal(lines, inc=1, device_id=(li, j), device_id_type=MESH)
 
     def share():
-        @pl.when(core == 0)
-        def _():
-            for g in range(len(GROUPS)):
-                sib_copy(g).start()
-
-    def lower(by):
-        if by == 1:
-            @pl.when(core == 1)
+        for g in range(len(GROUPS)):
+            sib_copy(g).start()
+
+    def lower():
+        for g in range(len(GROUPS)):
+            sib_copy(g).wait_recv()
+        chip_sum[...] = own_sum[...] + sib_sum[...]
+        for c in range(chips - 1):
+            @pl.when(chip == c)
             def _():
                 for g in range(len(GROUPS)):
-                    sib_copy(g).wait_recv()
-                chip_sum[...] = own_sum[...] + sib_sum[...]
-
-        @pl.when((core == 1) & (chip + by < chips))
-        def _():
-            for g in range(len(GROUPS)):
-                for to_core in range(2):
-                    low_copy(g, by, to_core).start()
+                    for to_core in range(2):
+                        for by in range(1, chips - c):
+                            low_copy(g, by, to_core).start()
 
     view_scale = -LOG2E * 2.0 / view_total
     light_scale = -LOG2E * 2.0 / light_total
@@ -234,15 +230,19 @@
 
     def low_chips():
         meet()
-        for by in range(1, chips):
-            lower(by)
-
+        lower()
+
+    def sibling():
+        meet()
+        share()
+
+    edge = (vx == 0) | (vy == 0)
     for k in range(chunks):
         sum_up(k)
-    pl.when(core == 0)(meet)
-    share()
+    pl.when((core == 0) & ~edge)(sibling)
     near_side(0)
     near_side(1)
+    pl.when((core == 0) & edge)(sibling)
     pl.when((core == 1) & (chip > 0))(low_chips)
     near_side(2)
     pl.when((core == 1) & (chip == 0))(low_chips)

time: 14.3 us -> 14.2 us (level)
  no operation moved by 1% of the time
where the time goes in v7:
time: 14.2 us; the launch traced here: 14 us
  Pallas kernels  13.4 us (94%)
  local copies, waits for them, and re-layouts  0.6 us (4%)
    pallas_call x1, Pallas kernels, body(): pl.pallas_call(functools.partial(kernel, lanes * light_count, cells * vie...  13.4 us
    unnamed x1, local copies, waits for them, and re-layouts  0.6 us

profile of v7, /device:TPU:96, one launch (start us, length us, event | category | flops | bytes accessed | tf_op | source)
XLA Modules:
  0.0 14.0 jit_solution(9963859353805704257)
XLA Ops:
  0.0 13.4 %shard_map.28 = f32[3,4,128]{2,1,0:T(4,128)S(1)} custom-call(bf16[128,64,128]{2,1,0:T(8,128)(2,1)} %x_hbm.1, f32[3,4]{1,0:T(4,128)} %coef_hbm.1), custom_call_target="tpu_custom_call" | custom-call | tf_op jit(solution)/shard_map/pallas_call | solution.py:296
  13.4 0.6 %copy.4 = f32[3,4,128]{2,1,0:T(4,128)} copy(f32[3,4,128]{2,1,0:T(4,128)S(1)} %shard_map.28) | data formatting | bytes 12288
